TPU v7x, 256 devices: a whole 4x4x8 slice. The times are simulated.
256 devices in a mesh: sub: 8 (over z), row: 2 (over core), col: 16 (over y, x).
Axes of the slice: x: 4, y: 4, z: 8, core: 2. Of those that a mesh axis runs over, the one named last changes fastest.
Arguments:
- factor_cols: bfloat16 [8, 2, 2048, 4096], P('sub', None, 'col', 'row'), may hold values from -0.09375 to 0.09375
- block_pattern: int32 [8, 16, 16], P('sub'), may hold values 0 or 1
- diag_inverse: float32 [8, 4096, 2048], P('sub', ('row', 'col')), may hold values from -1 to 2
- coupling_cols: bfloat16 [8, 2, 2048, 1024], P('sub', 'row', 'col'), may hold values from -0.09375 to 0.09375
- separator_rows: int32 [8, 1024], P('sub'), may hold values from 0 to 1535, as said below
- root_inverse: float32 [1536, 1536], P('col'), may hold values from -1 to 2
- right_side: float32 [8, 4096, 128], P('sub', 'row'), may hold values from -6 to 6
- root_right: float32 [1536, 128], P('col'), may hold values from -6 to 6
Outputs:
- solution: float32 [8, 4096, 128], P('sub', ('row', 'col'))
- root_solution: float32 [1536, 128], P('col')
Inputs may be any that keep to these rules, and one draw needn't show every extreme that they name: `separator_rows`: within one section the 1024 entries are distinct.
All inputs are finite; a program needn't handle non-finite values. No bound on the sum of `block_pattern` on one device may be relied on, other than what follows from the above.
Results may differ from a plain program's by a relative error of at most 0.003.
Values may be sent and summed in bfloat16 or wider, within the bound.
No kernel may reach another device: no remote copies, remote signals or barrier semaphores. Data moves between devices by JAX's collectives and lax.ppermute only.
A program may use at most 64 MiB of HBM per device.

v0:
```python
import jax
import jax.numpy as jnp
from jax import lax
from jax.sharding import PartitionSpec as P

BLOCK = 256
SEPARATOR = 1536
precise = lax.Precision.HIGHEST
first_axes = (((0,), (0,)), ((), ()))


def spread(block, axis, source):
    block = jnp.where(lax.axis_index(axis) == source, block, jnp.zeros_like(block))
    return lax.psum(block, axis)


def shards(
    factor_cols,
    block_pattern,
    diag_inverse,
    coupling_cols,
    separator_rows,
    root_inverse,
    right_side,
    root_right,
):
    factor = factor_cols[0]
    table = block_pattern[0]
    inverse = diag_inverse[0]
    couple_own = coupling_cols[0, 0]
    right_rows = right_side[0]
    rows_sep = separator_rows[0]
    panel_count, col_width, panel_rows = factor.shape
    sources = right_rows.shape[1]
    block_count = table.shape[1]
    row_id = lax.axis_index("row")
    col_id = lax.axis_index("col")
    sub_id = lax.axis_index("sub")
    own_blocks = lax.dynamic_slice_in_dim(
        table, row_id * (panel_rows // BLOCK), panel_rows // BLOCK, 0
    ).astype(jnp.float32)
    row_mask = jnp.repeat(own_blocks, BLOCK, axis=0)
    col_pos = (
        jnp.arange(panel_count)[:, None] * panel_rows
        + col_id * col_width
        + jnp.arange(col_width)[None, :]
    )
    selector = (jnp.arange(block_count)[:, None, None] == (col_pos // BLOCK)[None]).astype(
        jnp.float32
    )
    pattern_mask = jnp.einsum("in,nqj->qji", row_mask, selector)
    below_mask = (jnp.arange(panel_count) < row_id).astype(jnp.float32)[:, None, None]
    masked = factor * (pattern_mask * below_mask).astype(jnp.bfloat16)
    zero_panel = jnp.zeros((panel_rows, sources), jnp.float32)
    zero_share = jnp.zeros((col_width, sources), jnp.float32)

    def forward(current, carried):
        accumulated, solved = carried
        panel_total = lax.psum(accumulated, "col")
        solved = lax.cond(
            row_id == current,
            lambda values: jnp.dot(
                inverse, right_rows - values, precision=precise, preferred_element_type=jnp.float32
            ),
            lambda values: solved,
            panel_total,
        )
        received = spread(solved.astype(jnp.bfloat16), "row", current)
        factor_now = lax.dynamic_index_in_dim(masked, current, 0, keepdims=False)
        accumulated = accumulated + lax.dot_general(
            factor_now, received, first_axes, preferred_element_type=jnp.float32
        )
        return (accumulated, solved)

    accumulated, solved = lax.fori_loop(0, panel_count, forward, (zero_panel, zero_share))
    own_low = solved.astype(jnp.bfloat16)
    sep_partial = lax.dot_general(
        couple_own, own_low, first_axes, preferred_element_type=jnp.float32
    )
    onehot = (jnp.arange(SEPARATOR)[:, None] == rows_sep[None, :]).astype(jnp.float32)
    mapped = jnp.dot(onehot, sep_partial, precision=precise, preferred_element_type=jnp.float32)
    share_rows = root_inverse.shape[0]
    slice_start = col_id * share_rows
    first_device = ((sub_id == 0) & (row_id == 0)).astype(jnp.float32)
    own_rows = (
        lax.dynamic_slice_in_dim(-mapped, slice_start, share_rows, 0) + first_device * root_right
    )
    root_term = lax.dynamic_update_slice_in_dim(-mapped, own_rows, slice_start, 0)
    root_rhs = lax.psum(root_term, ("sub", "row", "col"))
    root_half = jnp.dot(
        root_inverse, root_rhs, precision=precise, preferred_element_type=jnp.float32
    )
    root_part = lax.psum_scatter(
        lax.dot_general(
            root_inverse,
            root_half,
            first_axes,
            precision=precise,
            preferred_element_type=jnp.float32,
        ),
        "col",
        scatter_dimension=0,
        tiled=True,
    )
    root_full = lax.all_gather(root_part.astype(jnp.bfloat16), "col", axis=0, tiled=True).astype(
        root_part.dtype
    )
    picked = lax.dot_general(
        onehot, root_full, first_axes, precision=precise, preferred_element_type=jnp.float32
    ).astype(jnp.bfloat16)
    couple_back = jnp.dot(couple_own, picked, preferred_element_type=jnp.float32)

    def backward(counter, carried):
        finished, panel_low = carried
        current = panel_count - 1 - counter
        factor_now = lax.dynamic_index_in_dim(masked, current, 0, keepdims=False)
        contribution = jnp.dot(factor_now, panel_low, preferred_element_type=jnp.float32)
        own_couple = couple_back * (row_id == current).astype(jnp.float32)
        summed = lax.psum(contribution + own_couple, "row")
        partial_value = lax.cond(
            row_id == current,
            lambda values: lax.dot_general(
                inverse,
                solved - values,
                first_axes,
                precision=precise,
                preferred_element_type=jnp.float32,
            ),
            lambda values: zero_panel,
            summed,
        )
        value = lax.psum_scatter(partial_value, "col", scatter_dimension=0, tiled=True)
        whole_low = lax.all_gather(value.astype(jnp.bfloat16), "col", axis=0, tiled=True)
        active = row_id == current
        finished = jnp.where(active, value, finished)
        panel_low = jnp.where(active, whole_low, panel_low)
        return (finished, panel_low)

    finished, panel_low = lax.fori_loop(
        0, panel_count, backward, (zero_share, zero_panel.astype(jnp.bfloat16))
    )
    return (finished[None], root_part)


def solution(mesh):
    return jax.shard_map(
        shards,
        mesh=mesh,
        in_specs=(
            P("sub", None, "col", "row"),
            P("sub", None, None),
            P("sub", ("row", "col"), None),
            P("sub", "row", "col", None),
            P("sub", None),
            P("col", None),
            P("sub", "row", None),
            P("col", None),
        ),
        out_specs=(P("sub", ("row", "col"), None), P("col", None)),
        check_vma=False,
    )
```

profile of v0, /device:TPU:32, one launch (start us, length us, event | category | flops | bytes accessed | tf_op | source)
XLA Modules:
  0.0 886.8 jit_solution(2642969435639359948)
XLA Ops:
  8.0 0.7 convert_bitcast_fusion
  8.8 0.1 copy.21
  9.1 2.8 fusion.15
  11.9 221.9 %while.37 = (s32[]{:T(128)}, f32[2048,128]{1,0:T(8,128)}, f32[128,128]{0,1:T(8,128)S(1)}, bf16[2,128,2048]{2,1,0:T(8,128)(2,1)}, s32[]{:T(128)}, /*index=5*/f32[...) while((s32[]{:T(128)}, f32[2048,128]{1,0:T(8,128)}, ...), condition=%wide.region_5.6_spmd.clone, body=%wide.region_0.5_spmd.clone.sunk | while | flops 470859776 | bytes 18612512 | solution.py:75
  12.0 1.1 broadcast_select_fusion.7
  13.1 103.1 %all-reduce.6.cloned.1.call-done = f32[2048,128]{1,0:T(8,128)} async-done(((f32[2048,128]{1,0:T(8,128)}), f32[2048,128]{1,0:T(8,128)}) %all-reduce.6.cloned.1.call-update) | async-done | bytes 1048592 | tf_op jit(solution)/shard_map/while/body/eval_jaxpr/psum | solution.py:59
  116.2 3.5 conditional.7
  116.2 3.5 convolution_bitcast_fusion.1
  119.7 3.4 psum.51
  123.1 2.4 convolution_add_fusion.4
  125.5 2.3 broadcast_select_fusion.7
  127.8 98.6 %all-reduce.6.cloned.1.call-done = f32[2048,128]{1,0:T(8,128)} async-done(((f32[2048,128]{1,0:T(8,128)}), f32[2048,128]{1,0:T(8,128)}) %all-reduce.6.cloned.1.call-update) | async-done | bytes 1048592 | tf_op jit(solution)/shard_map/while/body/eval_jaxpr/psum | solution.py:59
  226.4 5.1 psum.51
  231.4 2.4 convolution_add_fusion.4
  233.8 0.2 fusion.19
  234.0 2.9 fusion.16
  237.0 0.9 copy-done.5
  238.0 252.3 %all-reduce.4.cloned.1.call-done = f32[1536,128]{1,0:T(8,128)} async-done(((f32[1536,128]{1,0:T(8,128)}), f32[1536,128]{1,0:T(8,128)}) %all-reduce.4.cloned.1.call-update) | async-done | bytes 786448 | tf_op jit(solution)/shard_map/psum | solution.py:89
  490.3 1.9 fusion.24
  492.2 0.8 convolution_bitcast_fusion.2
  493.0 1.2 copy.27
  494.2 0.1 copy.24
  494.3 79.0 %reduce-scatter.5.cloned.1.call-done = f32[96,128]{1,0:T(8,128)} async-done(((f32[1536,128]{1,0:T(8,128)}), f32[96,128]{1,0:T(8,128)}) %reduce-scatter.5.cloned.1.call-update) | async-done | bytes 49168 | tf_op jit(solution)/shard_map/reduce_scatter | solution.py:93
  573.4 0.8 convert_element_type.87
  574.2 23.4 %all_gather.13 = bf16[1536,128]{1,0:T(8,128)(2,1)S(1)} all-gather(bf16[96,128]{1,0:T(8,128)(2,1)S(1)} %convert_element_type.87), channel_id=1, replica_groups=mesh['sub'=8,'row'=2,'col'=16] {'col'}, dimensions={0}, use_global_device_ids=true | all-gather | bytes 417792 | tf_op jit(solution)/shard_map/all_gather | solution.py:105
  597.6 1.8 fusion.17
  599.4 0.3 convolution_bitcast_fusion.3
  599.6 0.1 copy.23
  599.7 278.9 %while.38 = (s32[]{:T(128)}, f32[128,128]{0,1:T(8,128)S(1)}, bf16[2048,128]{0,1:T(8,128)(2,1)S(1)}, s32[]{:T(128)}, bf16[2,128,2048]{2,1,0:T(8,128)(2,1)}, /*ind...) while((s32[]{:T(128)}, f32[128,128]{0,1:T(8,128)S(1)}, ...), condition=%wide.region_13.14_spmd.clone, body=%wide.region_8.13_spmd.clone.sunk | while | flops 470663168 | bytes 13697360 | solution.py:139
  599.8 2.0 convolution_add_fusion.5
  601.9 29.3 %all-reduce.8.cloned.1.call-done = f32[128,128]{1,0:T(8,128)} async-done(((f32[128,128]{1,0:T(8,128)}), f32[128,128]{1,0:T(8,128)}) %all-reduce.8.cloned.1.call-update) | async-done | bytes 65552 | tf_op jit(solution)/shard_map/while/body/eval_jaxpr/psum | solution.py:119
  631.2 0.1 conditional.8
  631.2 0.1 broadcast_in_dim.1
  631.3 1.0 copy-done.3
  632.3 81.8 %reduce-scatter.7.cloned.1.call-done = f32[128,128]{0,1:T(8,128)} async-done(((f32[2048,128]{0,1:T(8,128)}), f32[128,128]{0,1:T(8,128)}) %reduce-scatter.7.cloned.1.call-update) | async-done | bytes 65552 | tf_op jit(solution)/shard_map/while/body/eval_jaxpr/reduce_scatter | solution.py:132
  714.2 0.9 fusion.43
  715.1 24.0 %all_gather.16 = bf16[2048,128]{0,1:T(8,128)(2,1)S(1)} all-gather(bf16[128,128]{0,1:T(8,128)(2,1)S(1)} %get-tuple-element.583), channel_id=1, replica_groups=mesh['sub'=8,'row'=2,'col'=16] {'col'}, dimensions={0}, use_global_device_ids=true | all-gather | bytes 557056 | tf_op jit(solution)/shard_map/while/body/eval_jaxpr/all_gather | solution.py:133
  739.1 0.2 broadcast_select_fusion.9
  739.4 2.0 convolution_add_fusion.5
  741.5 29.0 %all-reduce.8.cloned.1.call-done = f32[128,128]{1,0:T(8,128)} async-done(((f32[128,128]{1,0:T(8,128)}), f32[128,128]{1,0:T(8,128)}) %all-reduce.8.cloned.1.call-update) | async-done | bytes 65552 | tf_op jit(solution)/shard_map/while/body/eval_jaxpr/psum | solution.py:119
  770.5 1.9 conditional.8
  770.5 1.9 convolution_bitcast_fusion
  772.4 1.0 copy-done.3
  773.4 80.0 %reduce-scatter.7.cloned.1.call-done = f32[128,128]{0,1:T(8,128)} async-done(((f32[2048,128]{0,1:T(8,128)}), f32[128,128]{0,1:T(8,128)}) %reduce-scatter.7.cloned.1.call-update) | async-done | bytes 65552 | tf_op jit(solution)/shard_map/while/body/eval_jaxpr/reduce_scatter | solution.py:132
  853.5 0.9 fusion.43
  854.4 24.0 %all_gather.16 = bf16[2048,128]{0,1:T(8,128)(2,1)S(1)} all-gather(bf16[128,128]{0,1:T(8,128)(2,1)S(1)} %get-tuple-element.583), channel_id=1, replica_groups=mesh['sub'=8,'row'=2,'col'=16] {'col'}, dimensions={0}, use_global_device_ids=true | all-gather | bytes 557056 | tf_op jit(solution)/shard_map/while/body/eval_jaxpr/all_gather | solution.py:133
  878.4 0.2 broadcast_select_fusion.9
  878.6 0.7 copy.25
  (46 shorter events, 0.7 us)
Async XLA Ops:
  8.0 482.3 %copy-start = (f32[96,1536]{1,0:T(8,128)S(1)}, f32[96,1536]{1,0:T(8,128)}, u32[]{:S(2)}) copy-start(f32[96,1536]{1,0:T(8,128)} %param.21) | copy-start | bytes 1769476
  9.1 2.8 copy-start.2
  11.9 221.9 %copy-start.4 = (bf16[1,1,128,1024]{3,2,1,0:T(8,128)(2,1)S(1)}, bf16[1,1,128,1024]{3,2,1,0:T(8,128)(2,1)}, u32[]{:S(2)}) copy-start(bf16[1,1,128,1024]{3,2,1,0:T(8,128)(2,1)} %param.19) | copy-start | bytes 786436
  11.9 222.1 %copy-start.7 = (s32[1,1024]{1,0:T(1,128)S(1)}, s32[1,1024]{1,0:T(1,128)}, u32[]{:S(2)}) copy-start(s32[1,1024]{1,0:T(1,128)} %param.20) | copy-start | bytes 12292
  11.9 104.2 %all-reduce.6.cloned.1.call-start = ((), (), s32[]{:S(2)}) async-start(), calls=%async_computation.4 | async-start | bytes 2097152 | tf_op jit(solution)/shard_map/while/body/eval_jaxpr/psum | solution.py:59
  116.2 6.9 copy-start.1
  125.5 100.9 %all-reduce.6.cloned.1.call-start = ((), (), s32[]{:S(2)}) async-start(), calls=%async_computation.4 | async-start | bytes 2097152 | tf_op jit(solution)/shard_map/while/body/eval_jaxpr/psum | solution.py:59
  226.4 5.1 copy-start.1
  233.8 256.5 %all-reduce.4.cloned.1.call-start = ((), (), s32[]{:S(2)}) async-start(), calls=%async_computation.2 | async-start | bytes 1572864 | tf_op jit(solution)/shard_map/psum | solution.py:89
  234.0 2.9 copy-start.6
  237.0 0.9 copy-start.5
  237.9 335.5 %reduce-scatter.5.cloned.1.call-start = ((), (), s32[]{:S(2)}) async-start(), calls=%async_computation.3 | async-start | bytes 835584 | tf_op jit(solution)/shard_map/reduce_scatter | solution.py:93
  599.8 31.4 %all-reduce.8.cloned.1.call-start = ((), (), s32[]{:S(2)}) async-start(), calls=%async_computation.5 | async-start | bytes 131072 | tf_op jit(solution)/shard_map/while/body/eval_jaxpr/psum | solution.py:119
  601.8 112.3 %reduce-scatter.7.cloned.1.call-start = ((), (), s32[]{:S(2)}) async-start(), calls=%async_computation.6 | async-start | bytes 1114112 | tf_op jit(solution)/shard_map/while/body/eval_jaxpr/reduce_scatter | solution.py:132
  631.3 1.0 copy-start.3
  739.4 31.1 %all-reduce.8.cloned.1.call-start = ((), (), s32[]{:S(2)}) async-start(), calls=%async_computation.5 | async-start | bytes 131072 | tf_op jit(solution)/shard_map/while/body/eval_jaxpr/psum | solution.py:119
  741.4 112.0 %reduce-scatter.7.cloned.1.call-start = ((), (), s32[]{:S(2)}) async-start(), calls=%async_computation.6 | async-start | bytes 1114112 | tf_op jit(solution)/shard_map/while/body/eval_jaxpr/reduce_scatter | solution.py:132
  772.4 1.0 copy-start.3
Sparse Core Ops, SparseCore 0:
  16.4 99.7 all-reduce.5
  129.9 96.4 all-reduce.5
  603.9 27.2 all-reduce.7
  635.0 79.1 reduce-scatter.6
  743.2 27.2 all-reduce.7
  774.3 79.1 reduce-scatter.6
Sparse Core Ops, SparseCore 1:
  239.7 250.5 all-reduce.3
  494.6 78.7 reduce-scatter.4
where the time goes:
time: 888 us; the launch traced here: 887 us
  waiting for transfers between devices  753 us (85%)
  blocking collectives  79.9 us (9%)
  matrix products  24.7 us (3%)
  between operations  15.7 us (2%)
    psum x1, waiting for transfers between devices, shards(): root_rhs = lax.psum(root_term, ('sub', 'row', 'col'))  252 us
    psum x2, waiting for transfers between devices, forward(): panel_total = lax.psum(accumulated, 'col')  202 us
    reduce_scatter x2, waiting for transfers between devices, backward(): lax.psum_scatter(partial_value, 'col', scatter_dimension=0, tiled=True)  162 us
    reduce_scatter x1, waiting for transfers between devices, shards(): lax.psum_scatter(lax.dot_general(root_inverse, root_half, first_axes, pre...  79 us
    psum x2, waiting for transfers between devices, backward(): summed = lax.psum(contribution + own_couple, 'row')  58.3 us
    all_gather x2, blocking collectives, backward(): lax.all_gather(value.astype(jnp.bfloat16), 'col', axis=0, tiled=True)  48.1 us
    all_gather x1, blocking collectives, shards(): lax.all_gather(root_part.astype(jnp.bfloat16), 'col', axis=0, tiled=True)  23.4 us
  transfers between devices with their start and end apart: 8, of which 8 were waited for; matrix products, arithmetic and copies ran while one was open for 0% of the time, Pallas kernels for 0%

commit v1 on v0

--- a/solution.py
+++ b/solution.py
@@ -7,6 +7,11 @@
 SEPARATOR = 1536
 precise = lax.Precision.HIGHEST
 first_axes = (((0,), (0,)), ((), ()))
+
+
+def axis_by_axis(x, first, second):
+    partial = lax.psum(x, first)
+    return lax.psum(partial, second)
 
 
 def spread(block, axis, source):
@@ -86,7 +91,7 @@
         lax.dynamic_slice_in_dim(-mapped, slice_start, share_rows, 0) + first_device * root_right
     )
     root_term = lax.dynamic_update_slice_in_dim(-mapped, own_rows, slice_start, 0)
-    root_rhs = lax.psum(root_term, ("sub", "row", "col"))
+    root_rhs = axis_by_axis(root_term, "sub", ("row", "col"))
     root_half = jnp.dot(
         root_inverse, root_rhs, precision=precise, preferred_element_type=jnp.float32
     )

time: 888 us -> 823 us (0.927)
  waiting for transfers between devices: 753 us -> 689 us
    psum x1 -> x2, waiting for transfers between devices: 252 us -> 189 us  [the longest x1 115 us: axis_by_axis(): return lax.psum(partial, second)]
  transfers between devices with their start and end apart: 8 -> 9, of which waited for: 8 -> 9; matrix products, arithmetic and copies ran while one was open for 0% -> 0% of each run, Pallas kernels for 0% -> 0%
where the time goes in v1:
time: 823 us; the launch traced here: 822 us
  waiting for transfers between devices  689 us (84%)
  blocking collectives  79.9 us (10%)
  matrix products  24.7 us (3%)
  between operations  15.8 us (2%)
    psum x2, waiting for transfers between devices, forward(): panel_total = lax.psum(accumulated, 'col')  202 us
    reduce_scatter x2, waiting for transfers between devices, backward(): lax.psum_scatter(partial_value, 'col', scatter_dimension=0, tiled=True)  162 us
    psum x1, waiting for transfers between devices, axis_by_axis(): return lax.psum(partial, second)  115 us
    reduce_scatter x1, waiting for transfers between devices, shards(): lax.psum_scatter(lax.dot_general(root_inverse, root_half, first_axes, pre...  77.9 us
    psum x1, waiting for transfers between devices, axis_by_axis(): partial = lax.psum(x, first)  73.4 us
    psum x2, waiting for transfers between devices, backward(): summed = lax.psum(contribution + own_couple, 'row')  58.3 us
    all_gather x2, blocking collectives, backward(): lax.all_gather(value.astype(jnp.bfloat16), 'col', axis=0, tiled=True)  48.1 us
    all_gather x1, blocking collectives, shards(): lax.all_gather(root_part.astype(jnp.bfloat16), 'col', axis=0, tiled=True)  23.4 us
  transfers between devices with their start and end apart: 9, of which 9 were waited for; matrix products, arithmetic and copies ran while one was open for 0% of the time, Pallas kernels for 0%

profile of v1, /device:TPU:32, one launch (start us, length us, event | category | flops | bytes accessed | tf_op | source)
XLA Modules:
  0.0 822.5 jit_solution(1459054851037543681)
XLA Ops:
  8.0 0.7 convert_bitcast_fusion
  9.1 2.8 fusion.15
  11.9 221.9 %while.37 = (s32[]{:T(128)}, f32[2048,128]{1,0:T(8,128)}, f32[128,128]{0,1:T(8,128)S(1)}, bf16[2,128,2048]{2,1,0:T(8,128)(2,1)}, s32[]{:T(128)}, /*index=5*/f32[...) while((s32[]{:T(128)}, f32[2048,128]{1,0:T(8,128)}, ...), condition=%wide.region_5.6_spmd.clone, body=%wide.region_0.5_spmd.clone.sunk | while | flops 470859776 | bytes 18612512 | solution.py:80
  12.0 1.1 broadcast_select_fusion.7
  13.1 103.1 %all-reduce.9.cloned.1.call-done = f32[2048,128]{1,0:T(8,128)} async-done(((f32[2048,128]{1,0:T(8,128)}), f32[2048,128]{1,0:T(8,128)}) %all-reduce.9.cloned.1.call-update) | async-done | bytes 1048592 | tf_op jit(solution)/shard_map/while/body/eval_jaxpr/psum | solution.py:64
  116.2 3.5 conditional.7
  116.2 3.5 convolution_bitcast_fusion.1
  119.7 3.4 psum.59
  123.1 2.4 convolution_add_fusion.4
  125.5 2.3 broadcast_select_fusion.7
  127.8 98.5 %all-reduce.9.cloned.1.call-done = f32[2048,128]{1,0:T(8,128)} async-done(((f32[2048,128]{1,0:T(8,128)}), f32[2048,128]{1,0:T(8,128)}) %all-reduce.9.cloned.1.call-update) | async-done | bytes 1048592 | tf_op jit(solution)/shard_map/while/body/eval_jaxpr/psum | solution.py:64
  226.3 5.1 psum.59
  231.4 2.4 convolution_add_fusion.4
  233.8 0.2 fusion.19
  234.0 2.9 fusion.16
  237.0 0.9 copy-done.5
  238.0 73.4 %all-reduce.5.cloned.1.call-done = f32[1536,128]{1,0:T(8,128)} async-done(((f32[1536,128]{1,0:T(8,128)}), f32[1536,128]{1,0:T(8,128)}) %all-reduce.5.cloned.1.call-update) | async-done | bytes 786448 | tf_op jit(solution)/shard_map/psum | solution.py:13
  311.5 115.4 %all-reduce.7.cloned.1.call-done = f32[1536,128]{1,0:T(8,128)} async-done(((f32[1536,128]{1,0:T(8,128)}), f32[1536,128]{1,0:T(8,128)}) %all-reduce.7.cloned.1.call-update) | async-done | bytes 786448 | tf_op jit(solution)/shard_map/psum | solution.py:14
  426.9 1.9 fusion.24
  428.8 0.8 convolution_bitcast_fusion.2
  429.6 1.2 copy.27
  430.9 0.1 copy.24
  431.0 77.9 %reduce-scatter.5.cloned.1.call-done = f32[96,128]{1,0:T(8,128)} async-done(((f32[1536,128]{1,0:T(8,128)}), f32[96,128]{1,0:T(8,128)}) %reduce-scatter.5.cloned.1.call-update) | async-done | bytes 49168 | tf_op jit(solution)/shard_map/reduce_scatter | solution.py:98
  508.9 0.8 convert_element_type.87
  509.7 23.4 %all_gather.13 = bf16[1536,128]{1,0:T(8,128)(2,1)S(1)} all-gather(bf16[96,128]{1,0:T(8,128)(2,1)S(1)} %convert_element_type.87), channel_id=1, replica_groups=mesh['sub'=8,'row'=2,'col'=16] {'col'}, dimensions={0}, use_global_device_ids=true | all-gather | bytes 417792 | tf_op jit(solution)/shard_map/all_gather | solution.py:110
  533.1 1.8 fusion.17
  534.9 0.3 convolution_bitcast_fusion.3
  535.1 0.1 copy.23
  535.2 278.9 %while.38 = (s32[]{:T(128)}, f32[128,128]{0,1:T(8,128)S(1)}, bf16[2048,128]{0,1:T(8,128)(2,1)S(1)}, s32[]{:T(128)}, bf16[2,128,2048]{2,1,0:T(8,128)(2,1)}, /*ind...) while((s32[]{:T(128)}, f32[128,128]{0,1:T(8,128)S(1)}, ...), condition=%wide.region_14.15_spmd.clone, body=%wide.region_9.14_spmd.clone.sunk | while | flops 470663168 | bytes 13697360 | solution.py:144
  535.3 2.0 convolution_add_fusion.5
  537.4 29.3 %all-reduce.11.cloned.1.call-done = f32[128,128]{1,0:T(8,128)} async-done(((f32[128,128]{1,0:T(8,128)}), f32[128,128]{1,0:T(8,128)}) %all-reduce.11.cloned.1.call-update) | async-done | bytes 65552 | tf_op jit(solution)/shard_map/while/body/eval_jaxpr/psum | solution.py:124
  566.7 0.1 conditional.8
  566.7 0.1 broadcast_in_dim.1
  566.8 1.0 copy-done.3
  567.8 81.8 %reduce-scatter.7.cloned.1.call-done = f32[128,128]{0,1:T(8,128)} async-done(((f32[2048,128]{0,1:T(8,128)}), f32[128,128]{0,1:T(8,128)}) %reduce-scatter.7.cloned.1.call-update) | async-done | bytes 65552 | tf_op jit(solution)/shard_map/while/body/eval_jaxpr/reduce_scatter | solution.py:137
  649.7 0.9 fusion.43
  650.6 24.0 %all_gather.16 = bf16[2048,128]{0,1:T(8,128)(2,1)S(1)} all-gather(bf16[128,128]{0,1:T(8,128)(2,1)S(1)} %get-tuple-element.583), channel_id=1, replica_groups=mesh['sub'=8,'row'=2,'col'=16] {'col'}, dimensions={0}, use_global_device_ids=true | all-gather | bytes 557056 | tf_op jit(solution)/shard_map/while/body/eval_jaxpr/all_gather | solution.py:138
  674.6 0.2 broadcast_select_fusion.9
  674.9 2.0 convolution_add_fusion.5
  677.0 29.0 %all-reduce.11.cloned.1.call-done = f32[128,128]{1,0:T(8,128)} async-done(((f32[128,128]{1,0:T(8,128)}), f32[128,128]{1,0:T(8,128)}) %all-reduce.11.cloned.1.call-update) | async-done | bytes 65552 | tf_op jit(solution)/shard_map/while/body/eval_jaxpr/psum | solution.py:124
  706.0 1.9 conditional.8
  706.0 1.9 convolution_bitcast_fusion
  707.9 1.0 copy-done.3
  708.9 80.0 %reduce-scatter.7.cloned.1.call-done = f32[128,128]{0,1:T(8,128)} async-done(((f32[2048,128]{0,1:T(8,128)}), f32[128,128]{0,1:T(8,128)}) %reduce-scatter.7.cloned.1.call-update) | async-done | bytes 65552 | tf_op jit(solution)/shard_map/while/body/eval_jaxpr/reduce_scatter | solution.py:137
  789.0 0.9 fusion.43
  789.9 24.0 %all_gather.16 = bf16[2048,128]{0,1:T(8,128)(2,1)S(1)} all-gather(bf16[128,128]{0,1:T(8,128)(2,1)S(1)} %get-tuple-element.583), channel_id=1, replica_groups=mesh['sub'=8,'row'=2,'col'=16] {'col'}, dimensions={0}, use_global_device_ids=true | all-gather | bytes 557056 | tf_op jit(solution)/shard_map/while/body/eval_jaxpr/all_gather | solution.py:138
  813.9 0.2 broadcast_select_fusion.9
  814.1 0.7 copy.25
  (49 shorter events, 0.8 us)
Async XLA Ops:
  8.0 418.9 %copy-start = (f32[96,1536]{1,0:T(8,128)S(1)}, f32[96,1536]{1,0:T(8,128)}, u32[]{:S(2)}) copy-start(f32[96,1536]{1,0:T(8,128)} %param.21) | copy-start | bytes 1769476
  9.1 2.8 copy-start.2
  11.9 221.9 %copy-start.4 = (bf16[1,1,128,1024]{3,2,1,0:T(8,128)(2,1)S(1)}, bf16[1,1,128,1024]{3,2,1,0:T(8,128)(2,1)}, u32[]{:S(2)}) copy-start(bf16[1,1,128,1024]{3,2,1,0:T(8,128)(2,1)} %param.19) | copy-start | bytes 786436
  11.9 222.1 %copy-start.7 = (s32[1,1024]{1,0:T(1,128)S(1)}, s32[1,1024]{1,0:T(1,128)}, u32[]{:S(2)}) copy-start(s32[1,1024]{1,0:T(1,128)} %param.20) | copy-start | bytes 12292
  11.9 104.2 %all-reduce.9.cloned.1.call-start = ((), (), s32[]{:S(2)}) async-start(), calls=%async_computation.5 | async-start | bytes 2097152 | tf_op jit(solution)/shard_map/while/body/eval_jaxpr/psum | solution.py:64
  116.2 6.9 copy-start.1
  125.5 100.9 %all-reduce.9.cloned.1.call-start = ((), (), s32[]{:S(2)}) async-start(), calls=%async_computation.5 | async-start | bytes 2097152 | tf_op jit(solution)/shard_map/while/body/eval_jaxpr/psum | solution.py:64
  226.3 5.1 copy-start.1
  233.8 77.6 %all-reduce.5.cloned.1.call-start = ((), (), s32[]{:S(2)}) async-start(), calls=%async_computation.2 | async-start | bytes 1572864 | tf_op jit(solution)/shard_map/psum | solution.py:13
  234.0 2.9 copy-start.6
  237.0 0.9 copy-start.5
  237.9 189.0 %all-reduce.7.cloned.1.call-start = ((), (), s32[]{:S(2)}) async-start(), calls=%async_computation.3 | async-start | bytes 1572864 | tf_op jit(solution)/shard_map/psum | solution.py:14
  311.4 197.4 %reduce-scatter.5.cloned.1.call-start = ((), (), s32[]{:S(2)}) async-start(), calls=%async_computation.4 | async-start | bytes 835584 | tf_op jit(solution)/shard_map/reduce_scatter | solution.py:98
  535.2 31.5 %all-reduce.11.cloned.1.call-start = ((), (), s32[]{:S(2)}) async-start(), calls=%async_computation.6 | async-start | bytes 131072 | tf_op jit(solution)/shard_map/while/body/eval_jaxpr/psum | solution.py:124
  537.3 112.3 %reduce-scatter.7.cloned.1.call-start = ((), (), s32[]{:S(2)}) async-start(), calls=%async_computation.7 | async-start | bytes 1114112 | tf_op jit(solution)/shard_map/while/body/eval_jaxpr/reduce_scatter | solution.py:137
  566.8 1.0 copy-start.3
  674.9 31.1 %all-reduce.11.cloned.1.call-start = ((), (), s32[]{:S(2)}) async-start(), calls=%async_computation.6 | async-start | bytes 131072 | tf_op jit(solution)/shard_map/while/body/eval_jaxpr/psum | solution.py:124
  676.9 112.0 %reduce-scatter.7.cloned.1.call-start = ((), (), s32[]{:S(2)}) async-start(), calls=%async_computation.7 | async-start | bytes 1114112 | tf_op jit(solution)/shard_map/while/body/eval_jaxpr/reduce_scatter | solution.py:137
  707.9 1.0 copy-start.3
Sparse Core Ops, SparseCore 0:
  16.4 99.7 all-reduce.8
  129.9 96.4 all-reduce.8
  539.4 27.2 all-reduce.10
  570.5 79.1 reduce-scatter.6
  678.7 27.2 all-reduce.10
  709.8 79.1 reduce-scatter.6
Sparse Core Ops, SparseCore 1:
  238.0 73.3 all-reduce.4
  314.8 112.0 all-reduce.6
  431.2 77.6 reduce-scatter.4
